TPU v7x, 32 devices: a whole 2x2x4 slice. The times are simulated.
32 devices in a mesh: row: 8 (over y, x, core), col: 4 (over z).
Axes of the slice: x: 2, y: 2, z: 4, core: 2. Of those that a mesh axis runs over, the one named last changes fastest.
Arguments:
- vectors: bfloat16 [32768, 64], P(('row', 'col')), may hold values from -6 to 6
- cotangent: bfloat16 [32768, 64], P(('row', 'col')), may hold values from -360 to 360, as said below
- gap_weights: float32 [64, 64], replicated, as said below
- row_tile: int32 [8, 4, 128], P('row', 'col'), may hold values from -1 to 31, as said below
- col_tile: int32 [8, 4, 128], P('row', 'col'), may hold values from -1 to 63, as said below
Outputs:
- tile_grads: bfloat16 [8, 4, 128, 128, 128], P('row', 'col')
Inputs may be any that keep to these rules, and one draw needn't show every extreme that they name: `cotangent`: fresh draw of one law: entries of order one times a row scale rising along the vertices and a column scale per eigenvector. `gap_weights`: Positive, within a factor of 5 of 0.00125 / sqrt(32768). Used slots come first in each cell and name distinct tiles there; row_tile and col_tile are -1 together in padding slots; some cell uses all 128 slots. `col_tile`: padding slots are -1, as in row_tile.
All inputs are finite; a program needn't handle non-finite values.
Results may differ from a plain program's by a relative error of at most 0.011.
Values may be sent and summed in bfloat16 or wider, within the bound.
No kernel may reach another device: no remote copies, remote signals or barrier semaphores. Data moves between devices by JAX's collectives and lax.ppermute only.
A program may use at most 64 MiB of HBM per device.

v0:
```python
import jax
import jax.numpy as jnp
from jax import lax
from jax.sharding import PartitionSpec as P


def split_scaled(scaled):
    scaled_hi = scaled.astype(jnp.bfloat16)
    scaled_lo = (scaled - scaled_hi.astype(jnp.float32)).astype(jnp.bfloat16)
    return (scaled_hi, scaled_lo)


def mixed_rows(vec_rows, halves):
    first = jnp.dot(vec_rows, halves[0], preferred_element_type=jnp.float32)
    second = jnp.dot(vec_rows, halves[1], preferred_element_type=jnp.float32)
    return (first + second).astype(jnp.bfloat16)


def body(vectors, cotangent, gap_weights, row_tile, col_tile):
    eig_count = vectors.shape[1]
    partial_gram = lax.dot_general(
        vectors, cotangent, (((0,), (0,)), ((), ())), preferred_element_type=jnp.float32
    )
    gram_total = lax.psum(partial_gram, ("row", "col"))
    halves = split_scaled(gap_weights * gram_total)
    packed = vectors.reshape(-1, 2 * eig_count)
    vec_rows = lax.all_gather(packed, "col", axis=0, tiled=True).reshape(-1, eig_count)
    row_all = jnp.concatenate([mixed_rows(vec_rows, halves), vec_rows], axis=1)
    vec_rows = lax.all_gather(packed, "row", axis=0, tiled=True).reshape(-1, eig_count)
    col_all = jnp.concatenate([vec_rows, mixed_rows(vec_rows, halves)], axis=1)
    side = 128
    row_blocks = row_all.reshape(-1, side, 2 * eig_count)
    col_blocks = col_all.reshape(-1, side, 2 * eig_count)
    slot_count = row_tile.shape[-1]
    rows_idx = row_tile.reshape(slot_count)
    cols_idx = col_tile.reshape(slot_count)
    left_blocks = jnp.take(row_blocks, jnp.maximum(rows_idx, 0), axis=0)
    right_blocks = jnp.take(col_blocks, jnp.maximum(cols_idx, 0), axis=0)
    product = jnp.einsum(
        "gik,gjk->gij", left_blocks, right_blocks, preferred_element_type=jnp.float32
    )
    kept_mask = (rows_idx >= 0)[:, None, None]
    tiles_out = jnp.where(kept_mask, product, 0.0).astype(jnp.bfloat16)
    return tiles_out.reshape(1, 1, slot_count, side, side)


def solution(mesh):
    return jax.shard_map(
        body,
        mesh=mesh,
        in_specs=(
            P(("row", "col"), None),
            P(("row", "col"), None),
            P(),
            P("row", "col", None),
            P("row", "col", None),
        ),
        out_specs=P("row", "col", None, None, None),
        check_vma=False,
    )
```

profile of v0, /device:TPU:0, one launch (start us, length us, event | category | flops | bytes accessed | tf_op | source)
XLA Modules:
  0.0 105.1 jit_solution(2647410268700761317)
XLA Ops:
  6.5 0.0 copy-start
  6.5 0.0 all-gather.2.cloned.1.call-start
  6.5 1.1 %copy.6 = bf16[1024,64]{1,0:T(8,128)(2,1)S(1)} copy(bf16[1024,64]{0,1:T(8,128)(2,1)} %param.5) | data formatting | bytes 262144 | tf_op args[0]
  7.7 0.0 copy-start.2
  7.7 0.8 reshape.73
  8.5 0.0 all-gather.2.cloned.1.call-update
  8.5 0.0 copy-start.3
  8.5 17.6 %all_gather.6 = bf16[2048,128]{1,0:T(8,128)(2,1)S(1)} all-gather(bf16[512,128]{1,0:T(8,128)(2,1)} %reshape.73), channel_id=1, replica_groups=mesh['row'=8,'col'=4] {'col'}, dimensions={0}, use_global_device_ids=true | all-gather | bytes 655360 | tf_op jit(solution)/shard_map/all_gather | solution.py:27
  26.1 0.4 reshape.74
  26.5 0.4 concatenate.17
  26.9 0.0 copy-done
  26.9 0.0 copy-done.2
  26.9 0.2 fusion.18
  27.1 40.9 %psum.7 = f32[64,64]{1,0:T(8,128)S(1)} all-reduce(f32[64,64]{1,0:T(8,128)S(1)} %fusion.18), channel_id=1, replica_groups=mesh['row'=8,'col'=4] {'row','col'}, use_global_device_ids=true, to_apply=%region_0.0 | all-reduce | flops 4096 | bytes 32768 | tf_op jit(solution)/shard_map/psum | solution.py:24
  68.1 0.0 copy-done.3
  68.1 0.5 fusion.17
  68.6 0.0 copy-start.4
  68.6 1.3 %fusion.3 = bf16[4096,64]{0,1:T(8,128)(2,1)} fusion(f32[64,4096]{1,0:T(8,128)S(1)} %fusion.17, bf16[64,64]{1,0:T(8,128)(2,1)S(1)} %subtract_convert_fusion, bf16[4096,64]{1,0:T(8,128)(2,1)S(1)} %reshape.74), kind=kOutput, calls=%fused_computation.8 | convolution fusion | flops 34078720 | bytes 2105344 | tf_op jit(solution)/shard_map/dot_general | solution.py:15
  69.9 1.5 %copy.9 = bf16[4096,64]{1,0:T(8,128)(2,1)S(1)} copy(bf16[4096,64]{0,1:T(8,128)(2,1)} %fusion.3) | data formatting | bytes 1048576 | tf_op jit(solution)/shard_map/concatenate | solution.py:28
  71.4 0.0 copy-done.4
  71.5 0.6 pad_maximum_fusion.1
  72.0 0.0 copy-start.5
  72.1 3.0 %gather_fusion = bf16[128,128,128]{2,1,0:T(8,128)(2,1)} fusion(bf16[32,128,128]{2,1,0:T(8,128)(2,1)S(1)} %pad_maximum_fusion.1, s32[1024]{0:T(1024)S(1)} %pad_clamp_fusion.1), kind=kCustom, calls=%fused_computation | custom fusion | bytes 8389120 | tf_op jit(solution)/shard_map/jit(_take)/gather | solution.py:37
  75.1 0.0 copy-done.5
  75.1 0.0 all-gather.2.cloned.1.call-done
  75.1 2.7 %reshape.75 = bf16[8192,64]{1,0:T(8,128)(2,1)S(1)} reshape(bf16[4096,128]{1,0:T(8,128)(2,1)} %all-gather.2.cloned.1.call-done) | data formatting | bytes 2097152 | tf_op jit(solution)/shard_map/reshape | solution.py:29
  77.9 0.9 fusion.16
  78.8 0.9 fusion.1
  79.7 0.0 copy-start.1
  79.7 1.8 %copy.10 = bf16[8192,64]{1,0:T(8,128)(2,1)} copy(bf16[8192,64]{0,1:T(8,128)(2,1)S(1)} %fusion.1) | data formatting | bytes 2097152 | tf_op jit(solution)/shard_map/concatenate | solution.py:30
  81.4 0.0 copy-done.1
  81.4 1.9 %concatenate.19 = bf16[64,128,64]{2,1,0:T(8,128)(2,1)} reshape(bf16[4096,128]{1,0:T(8,128)(2,1)S(1)} %copy-done.1) | data formatting | bytes 2097152 | tf_op jit(solution)/shard_map/concatenate | solution.py:30
  83.3 3.4 %pad_maximum_fusion = bf16[64,128,128]{2,1,0:T(8,128)(2,1)S(1)} fusion(bf16[64,128,64]{2,1,0:T(8,128)(2,1)} %bitcast.26, bf16[64,128,64]{2,1,0:T(8,128)(2,1)} %concatenate.19), kind=kLoop, calls=%fused_computation.15 | loop fusion | flops 4194304 | bytes 4194304 | tf_op jit(solution)/shard_map/concatenate | solution.py:30
  86.7 3.1 %gather_fusion.1 = bf16[128,128,128]{2,1,0:T(8,128)(2,1)} fusion(bf16[64,128,128]{2,1,0:T(8,128)(2,1)S(1)} %pad_maximum_fusion, s32[1024]{0:T(1024)S(1)} %pad_clamp_fusion), kind=kCustom, calls=%fused_computation.1 | custom fusion | bytes 8389120 | tf_op jit(solution)/shard_map/jit(_take)/gather | solution.py:38
  89.7 8.6 %fusion.4 = bf16[1,1,128,128,128]{4,3,2,1,0:T(8,128)(2,1)} fusion(pred[128]{0:T(512)(128)(4,1)S(1)} %get-tuple-element.6, bf16[128,128,128]{2,1,0:T(8,128)(2,1)} %gather_fusion.1, pred[128]{0:T(512)(128)(4,1)S(1)} %get-tuple-element.7, bf16[128,128,128]{2,1,0:T(8,128)(2,1)} %gather_fusion, pred[128]{0:T(512)(128)(4,1)S(1)} %get-tuple-element.5), kind=kOutput, calls=%fused_computation.9 | convolution fusion | flops 545259520 | bytes 12583296 | tf_op jit(solution)/shard_map/gik,gjk->gij/dot_general | solution.py:39
  (6 shorter events, 0.0 us)
Async XLA Ops:
  6.5 20.4 %copy-start = (bf16[1024,64]{0,1:T(8,128)(2,1)S(1)}, bf16[1024,64]{0,1:T(8,128)(2,1)}, u32[]{:S(2)}) copy-start(bf16[1024,64]{0,1:T(8,128)(2,1)} %param.6) | copy-start | bytes 393220
  6.5 68.6 %all-gather.2.cloned.1.call-start = ((), (), s32[]{:S(2)}) async-start(), calls=%async_computation | async-start | bytes 1179648 | tf_op jit(solution)/shard_map/all_gather | solution.py:29
  7.7 19.3 %copy-start.2 = (bf16[1024,64]{0,1:T(8,128)(2,1)S(1)}, bf16[1024,64]{0,1:T(8,128)(2,1)}, u32[]{:S(2)}) copy-start(bf16[1024,64]{0,1:T(8,128)(2,1)} %param.5) | copy-start | bytes 393220
  8.5 59.6 %copy-start.3 = (f32[64,64]{1,0:T(8,128)S(1)}, f32[64,64]{1,0:T(8,128)}, u32[]{:S(2)}) copy-start(f32[64,64]{1,0:T(8,128)} %param.7) | copy-start | bytes 49156
  68.6 2.8 %copy-start.4 = (s32[1,1,128]{2,1,0:T(1,128)S(1)}, s32[1,1,128]{2,1,0:T(1,128)}, u32[]{:S(2)}) copy-start(s32[1,1,128]{2,1,0:T(1,128)} %param.8) | copy-start | bytes 1540
  72.0 3.0 %copy-start.5 = (s32[1,1,128]{2,1,0:T(1,128)S(1)}, s32[1,1,128]{2,1,0:T(1,128)}, u32[]{:S(2)}) copy-start(s32[1,1,128]{2,1,0:T(1,128)} %param.9) | copy-start | bytes 1540
  79.7 1.8 %copy-start.1 = (bf16[4096,128]{1,0:T(8,128)(2,1)S(1)}, bf16[4096,128]{1,0:T(8,128)(2,1)}, u32[]{:S(2)}) copy-start(bf16[4096,128]{1,0:T(8,128)(2,1)} %all-gather.2.cloned.1.call-done) | copy-start | bytes 3145732
Sparse Core Ops, SparseCore 0:
  9.2 26.1 all-gather.1
where the time goes:
time: 105 us
  blocking collectives  58.5 us (56%)
  local copies, waits for them, and re-layouts  16.7 us (16%)
  between operations  13.6 us (13%)
  matrix products  12.3 us (12%)
  other arithmetic  4 us (4%)
    psum x1, blocking collectives, body(): gram_total = lax.psum(partial_gram, ('row', 'col'))  40.9 us
    all_gather x1, blocking collectives, body(): lax.all_gather(packed, 'col', axis=0, tiled=True).reshape(-1, eig_count)  17.6 us
    dot_general x1, matrix products, body(): jnp.einsum('gik,gjk->gij', left_blocks, right_blocks, preferred_element_t...  8.57 us
    concatenate x2, local copies, waits for them, and re-layouts, body(): col_all = jnp.concatenate([vec_rows, mixed_rows(vec_rows, halves)], axis=1)  3.61 us
    concatenate x1, other arithmetic, body(): col_all = jnp.concatenate([vec_rows, mixed_rows(vec_rows, halves)], axis=1)  3.37 us
    gather x1, local copies, waits for them, and re-layouts, body(): right_blocks = jnp.take(col_blocks, jnp.maximum(cols_idx, 0), axis=0)  3.07 us
    gather x1, local copies, waits for them, and re-layouts, body(): left_blocks = jnp.take(row_blocks, jnp.maximum(rows_idx, 0), axis=0)  3.03 us
    reshape x1, local copies, waits for them, and re-layouts, body(): lax.all_gather(packed, 'row', axis=0, tiled=True).reshape(-1, eig_count)  2.75 us
  transfers between devices with their start and end apart: 1, of which 0 were waited for; matrix products, arithmetic and copies ran while one was open for 8% of the time, Pallas kernels for 0%

commit v1 on v0

--- a/solution.py
+++ b/solution.py
@@ -21,7 +21,7 @@
     partial_gram = lax.dot_general(
         vectors, cotangent, (((0,), (0,)), ((), ())), preferred_element_type=jnp.float32
     )
-    gram_total = lax.psum(partial_gram, ("row", "col"))
+    gram_total = jnp.sum(lax.all_gather(partial_gram, ("row", "col")), axis=0)
     halves = split_scaled(gap_weights * gram_total)
     packed = vectors.reshape(-1, 2 * eig_count)
     vec_rows = lax.all_gather(packed, "col", axis=0, tiled=True).reshape(-1, eig_count)

time: 105 us -> 149 us (1.42)
  blocking collectives: 58.5 us -> 99.9 us
    all_gather x0 -> x1, blocking collectives: none -> 84 us  [body(): gram_total = jnp.sum(lax.all_gather(partial_gram, ('row', 'col')), axis=0)]
    psum x1 -> x0, blocking collectives: 40.9 us -> none  [body(): gram_total = lax.psum(partial_gram, ('row', 'col'))]
    all_gather x1, blocking collectives: 17.6 us -> 15.9 us  [body(): lax.all_gather(packed, 'col', axis=0, tiled=True).reshape(-1, eig_count)]
  transfers between devices with their start and end apart: 1 -> 1, of which waited for: 0 -> 0; matrix products, arithmetic and copies ran while one was open for 8% -> 7% of each run, Pallas kernels for 0% -> 0%
where the time goes in v1:
time: 149 us
  blocking collectives  99.9 us (67%)
  local copies, waits for them, and re-layouts  16.7 us (11%)
  between operations  13.5 us (9%)
  matrix products  13.2 us (9%)
  other arithmetic  5.32 us (4%)
    all_gather x1, blocking collectives, body(): gram_total = jnp.sum(lax.all_gather(partial_gram, ('row', 'col')), axis=0)  84 us
    all_gather x1, blocking collectives, body(): lax.all_gather(packed, 'col', axis=0, tiled=True).reshape(-1, eig_count)  15.9 us
    dot_general x1, matrix products, body(): jnp.einsum('gik,gjk->gij', left_blocks, right_blocks, preferred_element_t...  8.57 us
    concatenate x2, local copies, waits for them, and re-layouts, body(): col_all = jnp.concatenate([vec_rows, mixed_rows(vec_rows, halves)], axis=1)  3.6 us
    concatenate x1, other arithmetic, body(): col_all = jnp.concatenate([vec_rows, mixed_rows(vec_rows, halves)], axis=1)  3.37 us
    gather x1, local copies, waits for them, and re-layouts, body(): right_blocks = jnp.take(col_blocks, jnp.maximum(cols_idx, 0), axis=0)  3.06 us
    gather x1, local copies, waits for them, and re-layouts, body(): left_blocks = jnp.take(row_blocks, jnp.maximum(rows_idx, 0), axis=0)  3.03 us
  transfers between devices with their start and end apart: 1, of which 0 were waited for; matrix products, arithmetic and copies ran while one was open for 7% of the time, Pallas kernels for 0%

profile of v1, /device:TPU:0, one launch (start us, length us, event | category | flops | bytes accessed | tf_op | source)
XLA Modules:
  0.0 148.7 jit_solution(17165392755428503363)
XLA Ops:
  6.5 0.0 copy-start
  6.5 0.0 all-gather.3.cloned.1.call-start
  6.5 1.1 copy.6
  7.7 0.8 reshape.73
  8.5 0.0 all-gather.3.cloned.1.call-update
  8.5 0.0 copy-done
  8.5 1.1 fusion.18
  9.6 84.0 %all-gather = f32[2048,64]{1,0:T(8,128)} all-gather(f32[64,64]{1,0:T(8,128)S(1)} %fusion.18), channel_id=2, replica_groups=mesh['row'=8,'col'=4] {'row','col'}, dimensions={0}, use_global_device_ids=true | all-gather | bytes 540672 | tf_op jit(solution)/shard_map/all_gather | solution.py:24
  93.6 15.9 %all_gather.14 = bf16[2048,128]{1,0:T(8,128)(2,1)S(1)} all-gather(bf16[512,128]{1,0:T(8,128)(2,1)} %reshape.73), channel_id=1, replica_groups=mesh['row'=8,'col'=4] {'col'}, dimensions={0}, use_global_device_ids=true | all-gather | bytes 655360 | tf_op jit(solution)/shard_map/all_gather | solution.py:27
  109.5 0.0 copy-start.2
  109.5 0.4 reshape.74
  109.9 0.4 concatenate.17
  110.3 1.3 reduce_sum.9
  111.7 0.0 copy-done.2
  111.7 0.5 fusion.17
  112.2 0.0 copy-start.3
  112.2 1.3 fusion.3
  113.5 1.5 %copy.9 = bf16[4096,64]{1,0:T(8,128)(2,1)S(1)} copy(bf16[4096,64]{0,1:T(8,128)(2,1)} %fusion.3) | data formatting | bytes 1048576 | tf_op jit(solution)/shard_map/concatenate | solution.py:28
  115.0 0.0 copy-done.3
  115.0 0.6 pad_maximum_fusion.1
  115.6 0.0 copy-start.4
  115.7 3.0 %gather_fusion = bf16[128,128,128]{2,1,0:T(8,128)(2,1)} fusion(bf16[32,128,128]{2,1,0:T(8,128)(2,1)S(1)} %pad_maximum_fusion.1, s32[1024]{0:T(1024)S(1)} %pad_clamp_fusion.1), kind=kCustom, calls=%fused_computation | custom fusion | bytes 8389120 | tf_op jit(solution)/shard_map/jit(_take)/gather | solution.py:37
  118.7 0.0 copy-done.4
  118.7 0.0 all-gather.3.cloned.1.call-done
  118.7 2.7 %reshape.75 = bf16[8192,64]{1,0:T(8,128)(2,1)S(1)} reshape(bf16[4096,128]{1,0:T(8,128)(2,1)} %all-gather.3.cloned.1.call-done) | data formatting | bytes 2097152 | tf_op jit(solution)/shard_map/reshape | solution.py:29
  121.5 0.9 fusion.16
  122.4 0.9 fusion.1
  123.2 0.0 copy-start.1
  123.2 1.8 %copy.10 = bf16[8192,64]{1,0:T(8,128)(2,1)} copy(bf16[8192,64]{0,1:T(8,128)(2,1)S(1)} %fusion.1) | data formatting | bytes 2097152 | tf_op jit(solution)/shard_map/concatenate | solution.py:30
  125.0 0.0 copy-done.1
  125.0 1.8 %concatenate.19 = bf16[64,128,64]{2,1,0:T(8,128)(2,1)} reshape(bf16[4096,128]{1,0:T(8,128)(2,1)S(1)} %copy-done.1) | data formatting | bytes 2097152 | tf_op jit(solution)/shard_map/concatenate | solution.py:30
  126.9 3.4 %pad_maximum_fusion = bf16[64,128,128]{2,1,0:T(8,128)(2,1)S(1)} fusion(bf16[64,128,64]{2,1,0:T(8,128)(2,1)} %bitcast.27, bf16[64,128,64]{2,1,0:T(8,128)(2,1)} %concatenate.19), kind=kLoop, calls=%fused_computation.15 | loop fusion | flops 4194304 | bytes 4194304 | tf_op jit(solution)/shard_map/concatenate | solution.py:30
  130.2 3.1 %gather_fusion.1 = bf16[128,128,128]{2,1,0:T(8,128)(2,1)} fusion(bf16[64,128,128]{2,1,0:T(8,128)(2,1)S(1)} %pad_maximum_fusion, s32[1024]{0:T(1024)S(1)} %pad_clamp_fusion), kind=kCustom, calls=%fused_computation.1 | custom fusion | bytes 8389120 | tf_op jit(solution)/shard_map/jit(_take)/gather | solution.py:38
  133.3 8.6 %fusion.4 = bf16[1,1,128,128,128]{4,3,2,1,0:T(8,128)(2,1)} fusion(pred[128]{0:T(512)(128)(4,1)S(1)} %get-tuple-element.6, bf16[128,128,128]{2,1,0:T(8,128)(2,1)} %gather_fusion.1, pred[128]{0:T(512)(128)(4,1)S(1)} %get-tuple-element.7, bf16[128,128,128]{2,1,0:T(8,128)(2,1)} %gather_fusion, pred[128]{0:T(512)(128)(4,1)S(1)} %get-tuple-element.5), kind=kOutput, calls=%fused_computation.9 | convolution fusion | flops 545259520 | bytes 12583296 | tf_op jit(solution)/shard_map/gik,gjk->gij/dot_general | solution.py:39
  (6 shorter events, 0.0 us)
Async XLA Ops:
  6.5 2.0 %copy-start = (bf16[1024,64]{0,1:T(8,128)(2,1)S(1)}, bf16[1024,64]{0,1:T(8,128)(2,1)}, u32[]{:S(2)}) copy-start(bf16[1024,64]{0,1:T(8,128)(2,1)} %param.6) | copy-start | bytes 393220
  6.5 112.2 %all-gather.3.cloned.1.call-start = ((), (), s32[]{:S(2)}) async-start(), calls=%async_computation | async-start | bytes 1179648 | tf_op jit(solution)/shard_map/all_gather | solution.py:29
  109.5 2.1 %copy-start.2 = (f32[64,64]{1,0:T(8,128)S(1)}, f32[64,64]{1,0:T(8,128)}, u32[]{:S(2)}) copy-start(f32[64,64]{1,0:T(8,128)} %param.7) | copy-start | bytes 49156
  112.2 2.8 %copy-start.3 = (s32[1,1,128]{2,1,0:T(1,128)S(1)}, s32[1,1,128]{2,1,0:T(1,128)}, u32[]{:S(2)}) copy-start(s32[1,1,128]{2,1,0:T(1,128)} %param.8) | copy-start | bytes 1540
  115.6 3.0 %copy-start.4 = (s32[1,1,128]{2,1,0:T(1,128)S(1)}, s32[1,1,128]{2,1,0:T(1,128)}, u32[]{:S(2)}) copy-start(s32[1,1,128]{2,1,0:T(1,128)} %param.9) | copy-start | bytes 1540
  123.2 1.8 %copy-start.1 = (bf16[4096,128]{1,0:T(8,128)(2,1)S(1)}, bf16[4096,128]{1,0:T(8,128)(2,1)}, u32[]{:S(2)}) copy-start(bf16[4096,128]{1,0:T(8,128)(2,1)} %all-gather.3.cloned.1.call-done) | copy-start | bytes 3145732
Sparse Core Ops, SparseCore 0:
  9.2 26.4 all-gather.2
